TPU v7x, 32 devices: a whole 2x2x4 slice. The times are simulated.
32 devices in a mesh: groups: 2 (over y), seq: 4 (over z), tp: 4 (over x, core).
Axes of the slice: x: 2, y: 2, z: 4, core: 2. Of those that a mesh axis runs over, the one named last changes fastest.
Arguments:
- queries: bfloat16 [8, 128, 5120], P('groups', 'seq', 'tp'), parts along dimension 0, may hold values from -40 to 40
- key_vectors: bfloat16 [8, 128, 5120], P('groups', 'seq', 'tp'), parts along dimension 0, may hold values from -40 to 40
- value_vectors: bfloat16 [8, 128, 5120], P('groups', 'seq', 'tp'), parts along dimension 0, may hold values from -6 to 6
- block_mask: int32 [40, 4, 4], P('tp'), may hold values from 0 to 1, as said below
- out_weight: bfloat16 [40, 128, 2560], P('tp', 'seq'), may hold values from -0.5 to 0.5
Outputs:
- projected: bfloat16 [8, 128, 2560], P('groups', 'seq', 'tp'), parts along dimension 0
There are 2 independent parts, one for each index of `groups`. A program takes and returns all parts, laid end to end along the dimension named above; an argument that names none is the same for every part. Nothing has to cross between parts.
Inputs may be any that keep to these rules, and one draw needn't show every extreme that they name: block_mask[h, b, b] = 1 for every head and block; every row of a head's mask has at most 4 ones, and every head has a row with exactly 4.
All inputs are finite; a program needn't handle non-finite values.
Results may differ from a plain program's by a relative error of at most 0.012.
Values may be sent and summed in bfloat16 or wider, within the bound.
No kernel may reach another device: no remote copies, remote signals or barrier semaphores. Data moves between devices by JAX's collectives and lax.ppermute only.
A program may use at most 64 MiB of HBM per device.

v0:
```python
import jax
import jax.numpy as jnp
import numpy as np
from jax import lax
from jax.sharding import PartitionSpec as P

KEYS = 28


def strip_tables(heads_local, blocks, slot_total):
    slot_ids = np.arange(slot_total)
    head_of = slot_ids * heads_local // slot_total
    per_head = np.bincount(head_of, minlength=heads_local)
    head_begin = np.cumsum(per_head) - per_head
    order_in_head = slot_ids - head_begin[head_of]
    head_share = per_head[head_of]
    first_block = order_in_head * blocks // head_share
    block_count = (order_in_head + 1) * blocks // head_share - first_block
    return (head_of, first_block, block_count)


def body(queries, key_vectors, value_vectors, block_mask, out_weight):
    rank_count = lax.axis_size("seq")
    my_rank = lax.axis_index("seq")
    block_total, row_share, feature_width = queries.shape
    heads_local = block_mask.shape[0]
    head_size = feature_width // heads_local
    block_rows = row_share * rank_count
    per_rank = (heads_local + rank_count - 1) // rank_count
    slot_total = rank_count * per_rank
    least_share = slot_total // heads_local
    strip_cap = ((block_total + least_share - 1) // least_share + 1) // 2 * 2
    key_cap = min(KEYS, block_total)
    head_of, first_block, block_count = strip_tables(heads_local, block_total, slot_total)
    slot_grid = np.arange(slot_total).reshape(rank_count, per_rank).T
    paired = jnp.concatenate(
        [
            key_vectors.reshape(block_total, row_share, heads_local, head_size),
            value_vectors.reshape(block_total, row_share, heads_local, head_size),
        ],
        axis=3,
    )
    send_heads = jnp.asarray(head_of[slot_grid].reshape(-1), jnp.int32)
    chosen = jnp.take(paired, send_heads, axis=2)
    chosen = chosen.reshape(block_total, row_share, per_rank, rank_count, 2 * head_size)
    outgoing_pairs = chosen.transpose(2, 0, 3, 1, 4).reshape(
        per_rank, block_total, block_rows, 2 * head_size
    )
    flat_queries = queries.reshape(block_total, row_share, heads_local, head_size).transpose(
        0, 2, 1, 3
    )
    flat_queries = flat_queries.reshape(block_total * heads_local, row_share, head_size)
    positions = np.arange(strip_cap)
    unit_block = first_block[slot_grid][:, None, :] + positions[None, :, None]
    is_live = positions[None, :, None] < block_count[slot_grid][:, None, :]
    unit_index = np.where(is_live, unit_block * heads_local + head_of[slot_grid][:, None, :], 0)
    picked = jnp.take(flat_queries, jnp.asarray(unit_index.reshape(-1), jnp.int32), axis=0)
    picked = jnp.where(
        jnp.asarray(is_live.reshape(-1))[:, None, None], picked, jnp.zeros_like(picked)
    )
    outgoing_queries = picked.reshape(per_rank, strip_cap, block_rows, head_size)
    strip_queries, strip_pairs = (
        lax.all_to_all(outgoing_queries, "seq", split_axis=2, concat_axis=2, tiled=True),
        lax.all_to_all(outgoing_pairs, "seq", split_axis=2, concat_axis=2, tiled=True),
    )
    my_slots = my_rank * per_rank + jnp.arange(per_rank, dtype=jnp.int32)
    my_heads = jnp.asarray(head_of, jnp.int32)[my_slots]
    my_first = jnp.asarray(first_block, jnp.int32)[my_slots]
    query_blocks = jnp.minimum(
        my_first[:, None] + jnp.arange(strip_cap, dtype=jnp.int32)[None, :], block_total - 1
    )
    mask_rows = block_mask[my_heads[:, None], query_blocks]
    column_ids = jnp.arange(block_total, dtype=jnp.int32)
    ranking = (1 - mask_rows) * block_total + column_ids
    key_pick = jnp.argsort(ranking, axis=-1)[..., :key_cap]
    key_live = jnp.take_along_axis(mask_rows, key_pick, axis=-1)
    group_total = per_rank * strip_cap // 2
    query_groups = strip_queries.reshape(group_total, 2, block_rows, head_size)
    pick_groups = key_pick.reshape(group_total, 2, key_cap)
    live_groups = key_live.reshape(group_total, 2, key_cap)
    slot_of_group = jnp.arange(group_total, dtype=jnp.int32) // (strip_cap // 2)
    score_scale = head_size ** (-0.5)

    def attend_group(inputs):
        query_tile, pick_tile, live_tile, slot_index = inputs
        pairs_here = strip_pairs[slot_index]
        gathered = pairs_here[pick_tile]
        scores = (
            jnp.einsum(
                "qid,qkjd->qikj",
                query_tile,
                gathered[..., :head_size],
                preferred_element_type=jnp.float32,
            )
            * score_scale
        )
        allowed = (live_tile > 0)[:, None, :, None]
        scores = jnp.where(allowed, scores, -jnp.inf)
        largest = jnp.max(scores, axis=(2, 3), keepdims=True)
        weights = jnp.exp(scores - largest)
        totals = jnp.sum(weights, axis=(2, 3))
        blended = jnp.einsum(
            "qikj,qkjd->qid",
            weights.astype(jnp.bfloat16),
            gathered[..., head_size:],
            preferred_element_type=jnp.float32,
        )
        return (blended / totals[..., None]).astype(jnp.bfloat16)

    strip_out = lax.map(attend_group, (query_groups, pick_groups, live_groups, slot_of_group))
    outgoing_out = strip_out.reshape(per_rank, strip_cap, block_rows, head_size)
    returned = lax.all_to_all(outgoing_out, "seq", split_axis=2, concat_axis=2, tiled=True)
    slot_mesh, step_mesh = np.meshgrid(np.arange(slot_total), positions, indexing="ij")
    live_slot = step_mesh < block_count[slot_mesh]
    placement_index = np.zeros((block_total, heads_local), np.int64)
    source_index = (
        slot_mesh % per_rank * strip_cap + step_mesh
    ) * rank_count + slot_mesh // per_rank
    placement_index[
        first_block[slot_mesh][live_slot] + step_mesh[live_slot], head_of[slot_mesh][live_slot]
    ] = source_index[live_slot]
    flat_back = returned.reshape(per_rank * strip_cap * rank_count, row_share, head_size)
    own_out = jnp.take(flat_back, jnp.asarray(placement_index.reshape(-1), jnp.int32), axis=0)
    own_out = own_out.reshape(block_total, heads_local, row_share, head_size)
    token_total = block_total * row_share
    token_out = own_out.transpose(0, 2, 1, 3).reshape(token_total, heads_local, head_size)
    partial_sum = jnp.einsum(
        "thd,hdo->to",
        token_out,
        lax.all_gather(out_weight, "seq", axis=1, tiled=True),
        preferred_element_type=jnp.float32,
    )
    summed = lax.psum_scatter(
        partial_sum.astype(jnp.bfloat16), "tp", scatter_dimension=1, tiled=True
    ).astype(jnp.float32)
    return summed.astype(jnp.bfloat16).reshape(block_total, row_share, summed.shape[1])


def solution(mesh):
    return jax.shard_map(
        body,
        mesh=mesh,
        in_specs=(
            P("groups", "seq", "tp"),
            P("groups", "seq", "tp"),
            P("groups", "seq", "tp"),
            P("tp", None, None),
            P("tp", "seq", None),
        ),
        out_specs=P("groups", "seq", "tp"),
        check_vma=False,
    )
```

profile of v0, /device:TPU:0, one launch (start us, length us, event | category | flops | bytes accessed | tf_op | source)
XLA Modules:
  0.0 199.6 jit_solution(3571935745771503848)
XLA Ops:
  6.5 1.2 reshape.189
  7.9 0.6 gather_fusion.4
  8.6 1.6 copy_select_fusion
  10.2 6.5 %all-to-all-start = ((bf16[3,4,128,128]{3,1,0,2:T(4,128)(2,1)}), bf16[3,4,128,128]{3,1,0,2:T(4,128)(2,1)S(1)}, u32[]{:S(2)}, u32[]{:S(2)}) async-start(bf16[3,4,128,128]{3,1,0,2:T(4,128)(2,1)} %copy_select_fusion), calls=%async_computation | async-start | bytes 786432 | tf_op jit(solution)/shard_map/all_to_all | solution.py:63
  16.7 0.7 all-gather.2.cloned.1.call-update
  17.5 0.6 gather_fusion.1
  18.1 0.6 gather_fusion.2
  19.0 0.6 gather_fusion.5
  19.7 1.5 copy.76
  21.2 7.2 %all-to-all-done = bf16[3,4,128,128]{3,1,0,2:T(4,128)(2,1)S(1)} async-done(((bf16[3,4,128,128]{3,1,0,2:T(4,128)(2,1)}), bf16[3,4,128,128]{3,1,0,2:T(4,128)(2,1)S(1)}, u32[]{:S(2)}, u32[]{:S(2)}) %all-to-all-start) | async-done | bytes 393248 | tf_op jit(solution)/shard_map/all_to_all | solution.py:63
  28.4 3.5 %all-to-all-start.1 = ((bf16[3,4,128,256]{3,1,0,2:T(4,128)(2,1)}), bf16[3,4,128,256]{3,1,0,2:T(4,128)(2,1)S(1)}, u32[]{:S(2)}, u32[]{:S(2)}) async-start(bf16[3,4,128,256]{3,1,0,2:T(4,128)(2,1)} %copy.76), calls=%async_computation.1 | async-start | bytes 1572864 | tf_op jit(solution)/shard_map/all_to_all | solution.py:64
  32.2 0.7 gather_fusion.3
  33.0 1.3 sort.17
  34.6 1.2 gather_fusion.7
  36.1 36.5 %all-to-all-done.1 = bf16[3,4,128,256]{3,1,0,2:T(4,128)(2,1)S(1)} async-done(((bf16[3,4,128,256]{3,1,0,2:T(4,128)(2,1)}), bf16[3,4,128,256]{3,1,0,2:T(4,128)(2,1)S(1)}, u32[]{:S(2)}, u32[]{:S(2)}) %all-to-all-start.1) | async-done | bytes 786464 | tf_op jit(solution)/shard_map/all_to_all | solution.py:64
  72.6 30.0 %while.10 = (s32[]{:T(128)}, bf16[6,2,128,128]{3,1,0,2:T(2,128)(2,1)}, s32[6,2,4]{2,1,0:T(2,128)S(1)}, bf16[6,2,128,128]{3,1,0,2:T(2,128)(2,1)S(1)}, s32[6]{0:T(...) while((s32[]{:T(128)}, ...), condition=%wide.region_4.5_spmd, body=%wide.region_1.4_spmd.sunk | while | flops 68092448 | bytes 4598155 | solution.py:110
  72.6 0.7 dynamic_slice.37
  75.6 0.6 gather_fusion
  76.6 0.3 fusion.34
  76.9 0.7 copy_dynamic-update-slice_fusion.2
  77.6 0.7 dynamic_slice.37
  80.6 0.6 gather_fusion
  81.6 0.3 fusion.34
  81.9 0.7 copy_dynamic-update-slice_fusion.2
  82.6 0.7 dynamic_slice.37
  85.6 0.6 gather_fusion
  86.6 0.3 fusion.34
  86.9 0.7 copy_dynamic-update-slice_fusion.2
  87.6 0.7 dynamic_slice.37
  90.6 0.6 gather_fusion
  91.6 0.3 fusion.34
  91.9 0.7 copy_dynamic-update-slice_fusion.2
  92.6 0.7 dynamic_slice.37
  95.6 0.6 gather_fusion
  96.6 0.3 fusion.34
  96.9 0.7 copy_dynamic-update-slice_fusion.2
  97.6 0.7 dynamic_slice.37
  100.6 0.6 gather_fusion
  101.6 0.3 fusion.34
  101.9 0.7 copy_dynamic-update-slice_fusion.2
  102.6 3.5 %all-to-all-start.2 = ((bf16[3,4,128,128]{3,1,0,2:T(4,128)(2,1)}), bf16[3,4,128,128]{3,1,0,2:T(4,128)(2,1)S(1)}, u32[]{:S(2)}, u32[]{:S(2)}) async-start(bf16[3,4,128,128]{3,1,0,2:T(4,128)(2,1)} %bitcast.24), calls=%async_computation.2 | async-start | bytes 786432 | tf_op jit(solution)/shard_map/all_to_all | solution.py:112
  106.2 23.9 %all-to-all-done.2 = bf16[3,4,128,128]{3,1,0,2:T(4,128)(2,1)S(1)} async-done(((bf16[3,4,128,128]{3,1,0,2:T(4,128)(2,1)}), bf16[3,4,128,128]{3,1,0,2:T(4,128)(2,1)S(1)}, u32[]{:S(2)}, u32[]{:S(2)}) %all-to-all-start.2) | async-done | bytes 393248 | tf_op jit(solution)/shard_map/all_to_all | solution.py:112
  130.2 0.6 gather_fusion.6
  130.8 34.5 %all-gather.2.cloned.1.call-done = bf16[10,128,2560]{2,1,0:T(8,128)(2,1)} async-done(((bf16[10,32,2560]{2,1,0:T(8,128)(2,1)}), bf16[10,128,2560]{2,1,0:T(8,128)(2,1)}) %all-gather.2.cloned.1.call-update) | async-done | bytes 6553616 | tf_op jit(solution)/shard_map/all_gather | solution.py:130
  165.3 3.9 %fusion.11 = bf16[128,2560]{1,0:T(8,128)(2,1)S(1)} fusion(bf16[128,10,128]{2,0,1:T(8,128)(2,1)S(1)} %bitcast.102, bf16[10,128,2560]{2,1,0:T(8,128)(2,1)} %all-gather.2.cloned.1.call-done), kind=kOutput, calls=%fused_computation.32 | convolution fusion | flops 839188480 | bytes 7536640 | tf_op jit(solution)/shard_map/thd,hdo->to/dot_general | solution.py:127
  169.2 1.1 copy.86
  170.3 20.7 %reduce-scatter.4.cloned.1.call-done = bf16[640,128]{1,0:T(8,128)(2,1)} async-done(((bf16[2560,128]{1,0:T(8,128)(2,1)}), bf16[640,128]{1,0:T(8,128)(2,1)}) %reduce-scatter.4.cloned.1.call-update) | async-done | bytes 163856
  191.0 1.7 copy.87
  (106 shorter events, 5.5 us)
Async XLA Ops:
  6.5 12.2 %copy-start = (bf16[4,32,1280]{2,1,0:T(8,128)(2,1)S(1)}, bf16[4,32,1280]{2,1,0:T(8,128)(2,1)}, u32[]{:S(2)}) copy-start(bf16[4,32,1280]{2,1,0:T(8,128)(2,1)} %param.14) | copy-start | bytes 983044
  6.5 1.3 copy-start.8
  6.5 2.0 copy-start.5
  8.6 8.9 %copy-start.2 = (s32[12]{0:T(128)S(1)}, s32[12]{0:T(128)}, u32[]{:S(2)}) copy-start(s32[12]{0:T(128)} %constant.133.clone) | copy-start | bytes 148
  10.2 7.9 %copy-start.1 = (s32[12]{0:T(128)S(1)}, s32[12]{0:T(128)}, u32[]{:S(2)}) copy-start(s32[12]{0:T(128)} %constant.134.clone) | copy-start | bytes 148
  10.2 8.5 %copy-start.7 = (s32[12]{0:T(128)S(1)}, s32[12]{0:T(128)}, u32[]{:S(2)}) copy-start(s32[12]{0:T(128)} %constant.199) | copy-start | bytes 148
  10.2 8.6 %copy-start.3 = (bf16[4,32,1280]{2,1,0:T(8,128)(2,1)S(1)}, bf16[4,32,1280]{2,1,0:T(8,128)(2,1)}, u32[]{:S(2)}) copy-start(bf16[4,32,1280]{2,1,0:T(8,128)(2,1)} %param.15) | copy-start | bytes 983044
  10.2 18.2 %all-to-all-start = ((bf16[3,4,128,128]{3,1,0,2:T(4,128)(2,1)}), bf16[3,4,128,128]{3,1,0,2:T(4,128)(2,1)S(1)}, u32[]{:S(2)}, u32[]{:S(2)}) async-start(bf16[3,4,128,128]{3,1,0,2:T(4,128)(2,1)} %copy_select_fusion), calls=%async_computation | async-start | bytes 786432 | tf_op jit(solution)/shard_map/all_to_all | solution.py:63
  16.7 148.6 %all-gather.2.cloned.1.call-start = ((), (), s32[]{:S(2)}) async-start(), calls=%async_computation.4 | async-start | bytes 8192000 | tf_op jit(solution)/shard_map/all_gather | solution.py:130
  19.7 12.4 %copy-start.4 = (s32[10,4,4]{0,2,1:T(4,128)S(1)}, s32[10,4,4]{0,2,1:T(4,128)}, u32[]{:S(2)}) copy-start(s32[10,4,4]{0,2,1:T(4,128)} %param.16) | copy-start | bytes 1924
  28.4 44.2 %all-to-all-start.1 = ((bf16[3,4,128,256]{3,1,0,2:T(4,128)(2,1)}), bf16[3,4,128,256]{3,1,0,2:T(4,128)(2,1)S(1)}, u32[]{:S(2)}, u32[]{:S(2)}) async-start(bf16[3,4,128,256]{3,1,0,2:T(4,128)(2,1)} %copy.76), calls=%async_computation.1 | async-start | bytes 1572864 | tf_op jit(solution)/shard_map/all_to_all | solution.py:64
  72.6 33.5 %copy-start.6 = (s32[40]{0:T(128)S(1)}, s32[40]{0:T(128)}, u32[]{:S(2)}) copy-start(s32[40]{0:T(128)} %constant.200) | copy-start | bytes 484
  102.6 27.5 %all-to-all-start.2 = ((bf16[3,4,128,128]{3,1,0,2:T(4,128)(2,1)}), bf16[3,4,128,128]{3,1,0,2:T(4,128)(2,1)S(1)}, u32[]{:S(2)}, u32[]{:S(2)}) async-start(bf16[3,4,128,128]{3,1,0,2:T(4,128)(2,1)} %bitcast.24), calls=%async_computation.2 | async-start | bytes 786432 | tf_op jit(solution)/shard_map/all_to_all | solution.py:112
  106.1 84.9 %reduce-scatter.4.cloned.1.call-start = ((), (), s32[]{:S(2)}) async-start(), calls=%async_computation.5 | async-start | bytes 819200
Sparse Core Ops, SparseCore 0:
  19.1 146.1 all-gather.1
  170.4 20.5 reduce-scatter.3
where the time goes:
time: 200 us
  waiting for transfers between devices  124 us (62%)
  local copies, waits for them, and re-layouts  25.2 us (13%)
  between operations  13.7 us (7%)
  starting transfers between devices  13.5 us (7%)
  loops' own time  12.7 us (6%)
  matrix products  7.13 us (4%)
  other arithmetic  3.88 us (2%)
    all_to_all x1, waiting for transfers between devices, body(): lax.all_to_all(outgoing_pairs, 'seq', split_axis=2, concat_axis=2, tiled=...  36.5 us
    all_gather x1, waiting for transfers between devices, body(): lax.all_gather(out_weight, 'seq', axis=1, tiled=True)  34.5 us
    all_to_all x1, waiting for transfers between devices, body(): lax.all_to_all(outgoing_out, 'seq', split_axis=2, concat_axis=2, tiled=True)  23.9 us
    unnamed x3, waiting for transfers between devices  21.5 us
    another operation x1, loops' own time, body(): lax.map(attend_group, (query_groups, pick_groups, live_groups, slot_of_gr...  12.7 us
    all_to_all x1, waiting for transfers between devices, body(): lax.all_to_all(outgoing_queries, 'seq', split_axis=2, concat_axis=2, tile...  7.18 us
    all_to_all x1, starting transfers between devices, body(): lax.all_to_all(outgoing_queries, 'seq', split_axis=2, concat_axis=2, tile...  6.48 us
    dynamic_slice x12, local copies, waits for them, and re-layouts, body(): lax.map(attend_group, (query_groups, pick_groups, live_groups, slot_of_gr...  4.29 us
  transfers between devices with their start and end apart: 5, of which 5 were waited for; matrix products, arithmetic and copies ran while one was open for 13% of the time, Pallas kernels for 0%

commit v1 on v0

--- a/solution.py
+++ b/solution.py
@@ -5,6 +5,18 @@
 from jax.sharding import PartitionSpec as P
 
 KEYS = 28
+
+
+def sent_to_each(x, axis, split, join):
+    ways, here = (lax.axis_size(axis), lax.axis_index(axis))
+    width = x.shape[split] // ways
+    turned = jnp.roll(x, -here * width, axis=split)
+    got = [lax.slice_in_dim(turned, 0, width, axis=split)]
+    for far in range(1, ways):
+        sent = lax.slice_in_dim(turned, far * width, (far + 1) * width, axis=split)
+        got.append(lax.ppermute(sent, axis, [(d, (d + far) % ways) for d in range(ways)]))
+    line = jnp.concatenate(got[::-1], axis=join)
+    return jnp.roll(line, (here + 1) * got[0].shape[join], axis=join)
 
 
 def strip_tables(heads_local, blocks, slot_total):
@@ -61,7 +73,7 @@
     outgoing_queries = picked.reshape(per_rank, strip_cap, block_rows, head_size)
     strip_queries, strip_pairs = (
         lax.all_to_all(outgoing_queries, "seq", split_axis=2, concat_axis=2, tiled=True),
-        lax.all_to_all(outgoing_pairs, "seq", split_axis=2, concat_axis=2, tiled=True),
+        sent_to_each(outgoing_pairs, "seq", 2, 2),
     )
     my_slots = my_rank * per_rank + jnp.arange(per_rank, dtype=jnp.int32)
     my_heads = jnp.asarray(head_of, jnp.int32)[my_slots]

time: 200 us -> 193 us (0.965)
  waiting for transfers between devices: 124 us -> 103 us
  starting transfers between devices: 13.5 us -> 28.3 us
  other arithmetic: 3.88 us -> 6.21 us
  local copies, waits for them, and re-layouts: 25.2 us -> 23.1 us
    all_to_all x1 -> x0, waiting for transfers between devices: 36.5 us -> none  [body(): lax.all_to_all(outgoing_pairs, 'seq', split_axis=2, concat_axis=2, tiled=...]
    all_to_all x1, starting transfers between devices: 3.46 us -> 17.8 us  [body(): lax.all_to_all(outgoing_out, 'seq', split_axis=2, concat_axis=2, tiled=True)]
    all_gather x1, waiting for transfers between devices: 34.5 us -> 47.6 us  [body(): lax.all_gather(out_weight, 'seq', axis=1, tiled=True)]
    ppermute x0 -> x3, waiting for transfers between devices: none -> 7.48 us  [sent_to_each(): lax.ppermute(sent, axis, [(d, (d + far) % ways) for d in range(ways)])]
    ppermute x0 -> x3, starting transfers between devices: none -> 6.25 us  [sent_to_each(): lax.ppermute(sent, axis, [(d, (d + far) % ways) for d in range(ways)])]
    all_to_all x1, waiting for transfers between devices: 7.18 us -> 2.13 us  [body(): lax.all_to_all(outgoing_queries, 'seq', split_axis=2, concat_axis=2, tile...]
    all_to_all x1 -> x0, starting transfers between devices: 3.51 us -> none  [body(): lax.all_to_all(outgoing_pairs, 'seq', split_axis=2, concat_axis=2, tiled=...]
    all_to_all x1, waiting for transfers between devices: 23.9 us -> 20.8 us  [body(): lax.all_to_all(outgoing_out, 'seq', split_axis=2, concat_axis=2, tiled=True)]
  transfers between devices with their start and end apart: 5 -> 7, of which waited for: 5 -> 5; matrix products, arithmetic and copies ran while one was open for 13% -> 14% of each run, Pallas kernels for 0% -> 0%
where the time goes in v1:
time: 193 us; the launch traced here: 192 us
  waiting for transfers between devices  103 us (53%)
  starting transfers between devices  28.3 us (15%)
  local copies, waits for them, and re-layouts  23.1 us (12%)
  between operations  13.6 us (7%)
  loops' own time  11.3 us (6%)
  matrix products  7.14 us (4%)
  other arithmetic  6.21 us (3%)
    all_gather x1, waiting for transfers between devices, body(): lax.all_gather(out_weight, 'seq', axis=1, tiled=True)  47.6 us
    unnamed x3, waiting for transfers between devices  24.5 us
    all_to_all x1, waiting for transfers between devices, body(): lax.all_to_all(outgoing_out, 'seq', split_axis=2, concat_axis=2, tiled=True)  20.8 us
    all_to_all x1, starting transfers between devices, body(): lax.all_to_all(outgoing_out, 'seq', split_axis=2, concat_axis=2, tiled=True)  17.8 us
    another operation x1, loops' own time, body(): lax.map(attend_group, (query_groups, pick_groups, live_groups, slot_of_gr...  11.3 us
    ppermute x3, waiting for transfers between devices, sent_to_each(): lax.ppermute(sent, axis, [(d, (d + far) % ways) for d in range(ways)])  7.48 us
    ppermute x3, starting transfers between devices, sent_to_each(): lax.ppermute(sent, axis, [(d, (d + far) % ways) for d in range(ways)])  6.25 us
    dynamic_update_slice x6, local copies, waits for them, and re-layouts, body(): lax.map(attend_group, (query_groups, pick_groups, live_groups, slot_of_gr...  4.27 us
  transfers between devices with their start and end apart: 7, of which 5 were waited for; matrix products, arithmetic and copies ran while one was open for 14% of the time, Pallas kernels for 0%

profile of v1, /device:TPU:0, one launch (start us, length us, event | category | flops | bytes accessed | tf_op | source)
XLA Modules:
  0.0 192.2 jit_solution(10101789413353211658)
XLA Ops:
  6.5 0.7 pad_clamp_fusion.2
  7.5 1.1 copy_bitcast_fusion.2
  8.7 0.6 gather_fusion.5
  9.4 0.4 fusion.19
  9.9 5.1 %collective-permute-start = (bf16[3,4,32,256]{3,2,1,0:T(8,128)(2,1)S(1)}, bf16[3,4,32,256]{3,2,1,0:T(8,128)(2,1)S(1)}, u32[]{:S(2)}, u32[]{:S(2)}) collective-permute-start(bf16[3,4,32,256]{3,2,1,0:T(8,128)(2,1)S(1)} %copy.95), channel_id=1, source_target_pairs={{0,12},{4,0},{8,4},{12,8},{1,13},{5,1},{9,5},{13,9},{2,14},{6,2},{... | collective-permute-start | bytes 589832 | tf_op jit(solution)/shard_map/ppermute | solution.py:17
  15.1 1.0 collective-permute-start.2
  16.5 0.6 gather_fusion.4
  17.2 1.6 copy_select_fusion
  18.8 4.2 %all-to-all-start = ((bf16[3,4,128,128]{3,1,0,2:T(4,128)(2,1)}), bf16[3,4,128,128]{3,1,0,2:T(4,128)(2,1)S(1)}, u32[]{:S(2)}, u32[]{:S(2)}) async-start(bf16[3,4,128,128]{3,1,0,2:T(4,128)(2,1)} %copy_select_fusion), calls=%async_computation | async-start | bytes 786432 | tf_op jit(solution)/shard_map/all_to_all | solution.py:75
  23.1 0.7 all-gather.2.cloned.1.call-update
  23.8 0.6 gather_fusion.1
  24.5 0.6 gather_fusion.2
  25.4 0.7 gather_fusion.3
  26.3 1.3 sort.17
  27.7 1.2 gather_fusion.7
  29.4 7.5 %collective-permute-done.1 = bf16[3,4,32,256]{3,2,1,0:T(8,128)(2,1)S(1)} collective-permute-done((bf16[3,4,32,256]{3,2,1,0:T(8,128)(2,1)S(1)}, bf16[3,4,32,256]{3,2,1,0:T(8,128)(2,1)S(1)}, u32[]{:S(2)}, u32[]{:S(2)}) %collective-permute-start.1) | collective-permute-done | bytes 196640 | tf_op jit(solution)/shard_map/ppermute | solution.py:17
  36.9 1.3 fusion.15
  38.1 2.1 %all-to-all-done = bf16[3,4,128,128]{3,1,0,2:T(4,128)(2,1)S(1)} async-done(((bf16[3,4,128,128]{3,1,0,2:T(4,128)(2,1)}), bf16[3,4,128,128]{3,1,0,2:T(4,128)(2,1)S(1)}, u32[]{:S(2)}, u32[]{:S(2)}) %all-to-all-start) | async-done | bytes 393248 | tf_op jit(solution)/shard_map/all_to_all | solution.py:75
  40.3 27.7 %while.10 = (s32[]{:T(128)}, bf16[6,2,128,128]{3,1,0,2:T(2,128)(2,1)}, s32[6,2,4]{2,1,0:T(2,128)S(1)}, bf16[6,2,128,128]{3,1,0,2:T(2,128)(2,1)S(1)}, s32[6]{0:T(...) while((s32[]{:T(128)}, ...), condition=%wide.region_4.6_spmd, body=%wide.region_1.0_spmd.sunk | while | flops 68092448 | bytes 4073867 | solution.py:122
  40.3 0.6 dynamic_slice.95
  42.8 0.6 gather_fusion
  44.2 0.7 copy_dynamic-update-slice_fusion.2
  44.9 0.6 dynamic_slice.95
  47.4 0.6 gather_fusion
  48.8 0.7 copy_dynamic-update-slice_fusion.2
  49.5 0.6 dynamic_slice.95
  52.1 0.6 gather_fusion
  53.1 0.3 fusion.44
  53.4 0.7 copy_dynamic-update-slice_fusion.2
  54.1 0.6 dynamic_slice.95
  56.7 0.6 gather_fusion
  57.7 0.3 fusion.44
  58.0 0.7 copy_dynamic-update-slice_fusion.2
  58.7 0.6 dynamic_slice.95
  61.3 0.6 gather_fusion
  62.3 0.3 fusion.44
  62.6 0.7 copy_dynamic-update-slice_fusion.2
  63.3 0.6 dynamic_slice.95
  65.9 0.6 gather_fusion
  67.2 0.7 copy_dynamic-update-slice_fusion.2
  67.9 17.8 %all-to-all-start.1 = ((bf16[3,4,128,128]{3,1,0,2:T(4,128)(2,1)}), bf16[3,4,128,128]{3,1,0,2:T(4,128)(2,1)S(1)}, u32[]{:S(2)}, u32[]{:S(2)}) async-start(bf16[3,4,128,128]{3,1,0,2:T(4,128)(2,1)} %bitcast.26), calls=%async_computation.1 | async-start | bytes 786432 | tf_op jit(solution)/shard_map/all_to_all | solution.py:124
  85.7 20.8 %all-to-all-done.1 = bf16[3,4,128,128]{3,1,0,2:T(4,128)(2,1)S(1)} async-done(((bf16[3,4,128,128]{3,1,0,2:T(4,128)(2,1)}), bf16[3,4,128,128]{3,1,0,2:T(4,128)(2,1)S(1)}, u32[]{:S(2)}, u32[]{:S(2)}) %all-to-all-start.1) | async-done | bytes 393248 | tf_op jit(solution)/shard_map/all_to_all | solution.py:124
  106.6 0.6 gather_fusion.6
  107.3 47.6 %all-gather.2.cloned.1.call-done = bf16[10,128,2560]{2,1,0:T(8,128)(2,1)} async-done(((bf16[10,32,2560]{2,1,0:T(8,128)(2,1)}), bf16[10,128,2560]{2,1,0:T(8,128)(2,1)}) %all-gather.2.cloned.1.call-update) | async-done | bytes 6553616 | tf_op jit(solution)/shard_map/all_gather | solution.py:142
  154.9 3.9 %fusion.11 = bf16[128,2560]{1,0:T(8,128)(2,1)S(1)} fusion(bf16[128,10,128]{2,0,1:T(8,128)(2,1)S(1)} %bitcast.100, bf16[10,128,2560]{2,1,0:T(8,128)(2,1)} %all-gather.2.cloned.1.call-done), kind=kOutput, calls=%fused_computation.31 | convolution fusion | flops 839188480 | bytes 7536640 | tf_op jit(solution)/shard_map/thd,hdo->to/dot_general | solution.py:139
  158.8 1.1 copy.89
  159.9 23.7 %reduce-scatter.4.cloned.1.call-done = bf16[640,128]{1,0:T(8,128)(2,1)} async-done(((bf16[2560,128]{1,0:T(8,128)(2,1)}), bf16[640,128]{1,0:T(8,128)(2,1)}) %reduce-scatter.4.cloned.1.call-update) | async-done | bytes 163856
  183.7 1.7 copy.90
  (107 shorter events, 6.3 us)
Async XLA Ops:
  6.5 1.0 copy-start
  9.8 6.4 %copy-start.3 = (bf16[4,32,1280]{2,1,0:T(8,128)(2,1)S(1)}, bf16[4,32,1280]{2,1,0:T(8,128)(2,1)}, u32[]{:S(2)}) copy-start(bf16[4,32,1280]{2,1,0:T(8,128)(2,1)} %param.15) | copy-start | bytes 983044
  9.8 6.6 %copy-start.7 = (s32[48]{0:T(128)S(1)}, s32[48]{0:T(128)}, u32[]{:S(2)}) copy-start(s32[48]{0:T(128)} %constant.218) | copy-start | bytes 580
  9.9 19.5 %collective-permute-start = (bf16[3,4,32,256]{3,2,1,0:T(8,128)(2,1)S(1)}, bf16[3,4,32,256]{3,2,1,0:T(8,128)(2,1)S(1)}, u32[]{:S(2)}, u32[]{:S(2)}) collective-permute-start(bf16[3,4,32,256]{3,2,1,0:T(8,128)(2,1)S(1)} %copy.95), channel_id=1, source_target_pairs={{0,12},{4,0},{8,4},{12,8},{1,13},{5,1},{9,5},{13,9},{2,14},{6,2},{... | collective-permute-start | bytes 589832 | tf_op jit(solution)/shard_map/ppermute | solution.py:17
  15.0 2.1 %copy-start.5 = (pred[3,4,4]{1,0,2:T(4,128)(4,1)S(1)}, pred[3,4,4]{1,0,2:T(4,128)(4,1)}, u32[]{:S(2)}) copy-start(pred[3,4,4]{1,0,2:T(4,128)(4,1)} %constant.165) | copy-start | bytes 148
  15.0 21.8 %collective-permute-start.1 = (bf16[3,4,32,256]{3,2,1,0:T(8,128)(2,1)S(1)}, bf16[3,4,32,256]{3,2,1,0:T(8,128)(2,1)S(1)}, u32[]{:S(2)}, u32[]{:S(2)}) collective-permute-start(bf16[3,4,32,256]{3,2,1,0:T(8,128)(2,1)S(1)} %copy.96), channel_id=1, source_target_pairs={{0,8},{4,12},{8,0},{12,4},{1,9},{5,13},{9,1},{13,5},{2,10},{6,14},... | collective-permute-start | bytes 589832 | tf_op jit(solution)/shard_map/ppermute | solution.py:17
  15.1 21.7 %collective-permute-start.2 = (bf16[3,4,32,256]{3,2,1,0:T(8,128)(2,1)S(1)}, bf16[3,4,32,256]{3,2,1,0:T(8,128)(2,1)S(1)}, u32[]{:S(2)}, u32[]{:S(2)}) collective-permute-start(bf16[3,4,32,256]{3,2,1,0:T(8,128)(2,1)S(1)} %copy.97), channel_id=1, source_target_pairs={{0,4},{4,8},{8,12},{12,0},{1,5},{5,9},{9,13},{13,1},{2,6},{6,10},{... | collective-permute-start | bytes 589832 | tf_op jit(solution)/shard_map/ppermute | solution.py:17
  17.2 6.6 %copy-start.2 = (s32[12]{0:T(128)S(1)}, s32[12]{0:T(128)}, u32[]{:S(2)}) copy-start(s32[12]{0:T(128)} %constant.153.clone) | copy-start | bytes 148
  18.8 5.6 %copy-start.1 = (s32[12]{0:T(128)S(1)}, s32[12]{0:T(128)}, u32[]{:S(2)}) copy-start(s32[12]{0:T(128)} %constant.154.clone) | copy-start | bytes 148
  18.8 6.5 %copy-start.4 = (s32[10,4,4]{0,2,1:T(4,128)S(1)}, s32[10,4,4]{0,2,1:T(4,128)}, u32[]{:S(2)}) copy-start(s32[10,4,4]{0,2,1:T(4,128)} %param.18) | copy-start | bytes 1924
  18.8 21.4 %all-to-all-start = ((bf16[3,4,128,128]{3,1,0,2:T(4,128)(2,1)}), bf16[3,4,128,128]{3,1,0,2:T(4,128)(2,1)S(1)}, u32[]{:S(2)}, u32[]{:S(2)}) async-start(bf16[3,4,128,128]{3,1,0,2:T(4,128)(2,1)} %copy_select_fusion), calls=%async_computation | async-start | bytes 786432 | tf_op jit(solution)/shard_map/all_to_all | solution.py:75
  23.1 131.9 %all-gather.2.cloned.1.call-start = ((), (), s32[]{:S(2)}) async-start(), calls=%async_computation.3 | async-start | bytes 8192000 | tf_op jit(solution)/shard_map/all_gather | solution.py:142
  40.3 45.4 %copy-start.6 = (s32[40]{0:T(128)S(1)}, s32[40]{0:T(128)}, u32[]{:S(2)}) copy-start(s32[40]{0:T(128)} %constant.220) | copy-start | bytes 484
  67.9 38.6 %all-to-all-start.1 = ((bf16[3,4,128,128]{3,1,0,2:T(4,128)(2,1)}), bf16[3,4,128,128]{3,1,0,2:T(4,128)(2,1)S(1)}, u32[]{:S(2)}, u32[]{:S(2)}) async-start(bf16[3,4,128,128]{3,1,0,2:T(4,128)(2,1)} %bitcast.26), calls=%async_computation.1 | async-start | bytes 786432 | tf_op jit(solution)/shard_map/all_to_all | solution.py:124
  85.7 98.0 %reduce-scatter.4.cloned.1.call-start = ((), (), s32[]{:S(2)}) async-start(), calls=%async_computation.4 | async-start | bytes 819200
Sparse Core Ops, SparseCore 0:
  25.4 129.4 all-gather.1
  160.0 23.5 reduce-scatter.3
